TPU v7x, 128 devices: a whole 4x4x4 slice. The times are simulated.
128 devices in a mesh: gx: 16 (over x, y), gy: 8 (over z, core).
Axes of the slice: x: 4, y: 4, z: 4, core: 2. Of those that a mesh axis runs over, the one named last changes fastest.
Arguments:
- volts: float32 [32, 4, 128, 1024], P(None, None, 'gx', 'gy'), may hold values from -6 to 6
- cap: float32 [4, 128, 1024], P(None, 'gx', 'gy'), may hold values from 0.05 to 1
- cond_x: float32 [4, 128, 1024], P(None, 'gx', 'gy'), may hold values from 0.5 to 2
- cond_y: float32 [4, 128, 1024], P(None, 'gx', 'gy'), may hold values from 0.5 to 2
- via: float32 [4, 128, 1024], P(None, 'gx', 'gy'), may hold values from 0.2 to 2
- waveforms: float32 [64, 64], replicated, may hold values from -6 to 6
- placement: int32 [1048576, 1], P(('gx', 'gy')), may hold values from 0 to 127; in each aligned block of 8192 rows (0 to 8191, 8192 to 16383, ...) at most 128 rows name the same one
- cells: int32 [1048576], P(('gx', 'gy')), may hold values from 0 to 1023
- wave_ids: int32 [1048576], P(('gx', 'gy')), may hold values from 0 to 63
- amps: float32 [1048576], P(('gx', 'gy')), may hold values from 0.5 to 4
Outputs:
- volts_out: float32 [32, 4, 128, 1024], P(None, None, 'gx', 'gy')
- residual: float32 [32, 4, 128, 1024], P(None, None, 'gx', 'gy')
Inputs may be any that keep to these rules, and one draw needn't show every extreme that they name: `placement`: in each device's block of 8192 rows no tile is named more than 128 times, a bound that some block reaches.
All inputs are finite; a program needn't handle non-finite values.
Results may differ from a plain program's by a relative error of at most 0.0029.
Values may be sent and summed in bfloat16 or wider, within the bound.
No kernel may reach another device: no remote copies, remote signals or barrier semaphores. Data moves between devices by JAX's collectives and lax.ppermute only.
A program may use at most 64 MiB of HBM per device.

v0:
```python
import functools
import jax
import jax.numpy as jnp
from jax import lax
from jax.sharding import Mesh
from jax.sharding import PartitionSpec as P

ITERS = 3
GX_GY = ("gx_0", "gx_1", "gy_0", "gy_1")
GX = ("gx_0", "gx_1")
GY = ("gy_0", "gy_1")


def with_halo(x, sides, width):
    edges = {}
    for axis, dim in sides:
        size, length = (lax.axis_size(axis), x.shape[dim])
        up = [(i, (i + 1) % size) for i in range(size - 1)]
        last = lax.slice_in_dim(x, length - width, length, axis=dim)
        initial = lax.slice_in_dim(x, 0, width, axis=dim)
        edges[dim] = (
            lax.ppermute(last, axis, up),
            lax.ppermute(initial, axis, [(b, a) for a, b in up]),
        )
    done = []
    for _, dim in sides:
        low, high = edges[dim]
        around = [(width, width) if d in done else (0, 0) for d in range(x.ndim)]
        x = jnp.concatenate([jnp.pad(low, around), x, jnp.pad(high, around)], axis=dim)
        done.append(dim)
    return x


def shifted(x, axis, by):
    length = lax.axis_size(axis)
    pairs = [(i, i + by) for i in range(length) if 0 <= i + by < length]
    return lax.ppermute(x, axis, pairs)


def by_axis(x, axes):
    return functools.reduce(lax.psum, axes, x)


def gram(left, right):
    left_rows = left.reshape(left.shape[0], -1)
    right_rows = right.reshape(right.shape[0], -1)
    return lax.dot_general(
        left_rows, right_rows, (((1,), (1,)), ((), ())), precision=lax.Precision.HIGHEST
    )


def combine(coef, field):
    return jnp.einsum("st,slxy->tlxy", coef, field, precision=lax.Precision.HIGHEST)


def spd_solve(matrix, right):
    factor = jnp.linalg.cholesky(matrix)
    return jax.scipy.linalg.cho_solve((factor, True), right)


def make_currents(waveforms, kinds, scales):
    table_hits = (
        jnp.arange(waveforms.shape[1], dtype=jnp.int32)[:, None] == kinds[None, :]
    ).astype(jnp.float32)
    picked = jnp.dot(waveforms, table_hits, precision=lax.Precision.HIGHEST)
    return (picked * scales[None, :]).astype(jnp.bfloat16)


def operate(field, cap, cond_x, cond_x_low, cond_y, cond_y_low, via, via_low):
    padded = with_halo(field, ((GX, 2), (GY, 3)), 1)
    zero_layer = jnp.zeros_like(field[:, :1])
    upper = jnp.concatenate([field[:, 1:], zero_layer], axis=1)
    lower = jnp.concatenate([zero_layer, field[:, :-1]], axis=1)
    result = cap * field
    result = result + cond_x * (field - padded[:, :, 2:, 1:-1])
    result = result + cond_x_low * (field - padded[:, :, :-2, 1:-1])
    result = result + cond_y * (field - padded[:, :, 1:-1, 2:])
    result = result + cond_y_low * (field - padded[:, :, 1:-1, :-2])
    result = result + via * (field - upper) + via_low * (field - lower)
    return result


def body(volts, cap, cond_x, cond_y, via, waveforms, placement, cells, wave_ids, amps):
    devices = lax.axis_size(GX_GY)
    scenarios = volts.shape[0]
    steps = waveforms.shape[0] // scenarios
    tile_x = volts.shape[2]
    tile_y = volts.shape[3]
    die_cells = tile_x * tile_y
    slots_all = 2 * cells.shape[0]
    capacity = slots_all // devices
    target = placement[:, 0]
    target_hits = (jnp.arange(devices, dtype=jnp.int32)[:, None] == target[None, :]).astype(
        jnp.int32
    )
    running = jnp.cumsum(target_hits, axis=1) - 1
    position = jnp.sum(target_hits * running, axis=0)
    slot_index = target * capacity + position
    currents = make_currents(waveforms, wave_ids, amps)
    packed = jnp.zeros((currents.shape[0], slots_all), jnp.bfloat16).at[:, slot_index].set(currents)
    cell_slots = jnp.zeros((1, slots_all), jnp.int32).at[0, slot_index].set(cells)
    arrived, cell_slots = (
        lax.all_to_all(packed, GX_GY, split_axis=1, concat_axis=1, tiled=True),
        lax.all_to_all(cell_slots, GX_GY, split_axis=1, concat_axis=1, tiled=True),
    )
    block_rows = min(1024, slots_all)
    block_count = slots_all // block_rows
    cell_line = jnp.arange(die_cells, dtype=jnp.int32)

    def add_block(turn, total):
        piece_values = lax.dynamic_slice_in_dim(arrived, turn * block_rows, block_rows, 1)
        piece_cells = lax.dynamic_slice_in_dim(cell_slots[0], turn * block_rows, block_rows, 0)
        one_hot = (piece_cells[:, None] == cell_line[None, :]).astype(jnp.bfloat16)
        return total + jnp.dot(piece_values, one_hot, preferred_element_type=jnp.float32)

    injected = lax.fori_loop(
        0, block_count, add_block, jnp.zeros((arrived.shape[0], die_cells), jnp.float32)
    )
    injected = injected.reshape(steps, scenarios, tile_x, tile_y)
    rim_x = shifted(cond_x[:, -1:, :], GX, 1)
    rim_y = shifted(cond_y[:, :, -1:], GY, 1)
    cond_x_low = jnp.concatenate([rim_x, cond_x[:, :-1, :]], axis=1)
    cond_y_low = jnp.concatenate([rim_y, cond_y[:, :, :-1]], axis=2)
    via_low = jnp.concatenate([jnp.zeros_like(via[:1]), via[:-1]], axis=0)

    def apply_grid(field):
        return operate(field, cap, cond_x, cond_x_low, cond_y, cond_y_low, via, via_low)

    voltage = volts
    residual = volts
    for step in range(steps):
        rhs = cap * voltage
        rhs = rhs.at[:, 0].add(-injected[step])
        iterate = voltage
        residual = rhs - apply_grid(iterate)
        direction = residual
        norm_gram = by_axis(gram(residual, residual), GX_GY)
        for sweep in range(ITERS):
            image = apply_grid(direction)
            curve_gram, cross_gram, image_gram = (
                by_axis(gram(direction, image), GX_GY),
                by_axis(gram(residual, image), GX_GY),
                by_axis(gram(image, image), GX_GY),
            )
            step_coef = spd_solve(curve_gram, norm_gram)
            iterate = iterate + combine(step_coef, direction)
            residual = residual - combine(step_coef, image)
            if sweep + 1 < ITERS:
                cross_term = jnp.dot(cross_gram, step_coef, precision=lax.Precision.HIGHEST)
                square_term = jnp.dot(
                    step_coef.T,
                    jnp.dot(image_gram, step_coef, precision=lax.Precision.HIGHEST),
                    precision=lax.Precision.HIGHEST,
                )
                new_gram = norm_gram - cross_term - cross_term.T + square_term
                turn_coef = spd_solve(norm_gram, new_gram)
                direction = residual + combine(turn_coef, direction)
                norm_gram = new_gram
        voltage = iterate
    return (voltage, residual)


def solution(mesh):
    finer = Mesh(mesh.devices.reshape(4, 4, 4, 2), ("gx_0", "gx_1", "gy_0", "gy_1"))
    in_specs = (
        P(None, None, GX, GY),
        P(None, GX, GY),
        P(None, GX, GY),
        P(None, GX, GY),
        P(None, GX, GY),
        P(),
        P(GX_GY, None),
        P(GX_GY),
        P(GX_GY),
        P(GX_GY),
    )
    out_specs = (P(None, None, GX, GY), P(None, None, GX, GY))
    return jax.shard_map(body, mesh=finer, in_specs=in_specs, out_specs=out_specs, check_vma=False)
```

profile of v0, /device:TPU:1, one launch (start us, length us, event | category | flops | bytes accessed | tf_op | source)
XLA Modules:
  0.0 691.4 jit_solution(8659340981578746071)
XLA Ops:
  12.3 23.6 %scatter_custom_fusion = bf16[64,16384]{0,1:T(8,128)(2,1)} fusion(s32[8192]{0:T(1024)S(1)} %bitcast.343, bf16[8192,64]{1,0:T(8,128)(2,1)S(1)} %copy.198, bf16[]{:T(256)} %constant.131.clone.1), kind=kCustom, calls=%fused_computation.19 | custom fusion | bytes 2097154 | tf_op jit(solution)/shard_map/scatter | solution.py:100
  40.8 11.5 %all-to-all-start = ((bf16[64,128,128]{2,0,1:T(8,128)(2,1)}), bf16[64,128,128]{2,0,1:T(8,128)(2,1)S(1)}, u32[]{:S(2)}, u32[]{:S(2)}) async-start(bf16[64,128,128]{2,0,1:T(8,128)(2,1)} %copy.199), calls=%async_computation | async-start | bytes 4194304 | tf_op jit(solution)/shard_map/all_to_all | solution.py:103
  70.1 31.2 %scatter_custom_fusion.1 = s32[16384]{0:T(1024)} fusion(s32[8192]{0:T(1024)S(1)} %broadcast_select_fusion, s32[8192]{0:T(1024)} %param.26, s32[]{:T(128)} %constant.129.clone.1), kind=kCustom, calls=%fused_computation.288 | custom fusion | bytes 66048
  129.6 43.1 %while.16 = (s32[]{:T(128)}, f32[64,1024]{1,0:T(8,128)}, bf16[64,16384]{1,0:T(8,128)(2,1)}, s32[1,16384]{1,0:T(1,128)S(1)}, s32[]{:T(128)}, /*index=5*/s32[]{:T(128)}, s32[]{:T(128)}, s32[]{:T(128)}) while((s32[]{:T(128)}, f32[64,1024]{1,0:T(8,128)}, bf16[64,16384]{1,0:T(8,128)(2,1)}, s32[1,16384]{1,0:T(1,128)S(1)}, s32[]{:T(128)}, ...), condition=%wide.region_6.7_spmd.clone, body=%wide.region_5.6_spmd.clone.sunk | while | flops 135397376 | bytes 667797 | solution.py:116
  190.3 16.8 %all-reduce.45 = (f32[32,32]{0,1:T(8,128)S(1)}, f32[32,32]{0,1:T(8,128)S(1)}, f32[32,32]{1,0:T(8,128)S(1)}) all-reduce(f32[32,32]{0,1:T(8,128)S(1)} %convolution_bitcast_fusion.18, f32[32,32]{0,1:T(8,128)S(1)} %convolution_bitcast_fusion.19, ...), channel_id=1, replica_groups=mesh['gx_0'=4,'gx_1'=4,'gy_0'=4,'gy_1'=2] {'gx_0'}, use_global_device_ids=true, to_apply=%region_13.15 | all-reduce | flops 3072 | bytes 24576 | tf_op jit(solution)/shard_map/psum | solution.py:41
  207.1 11.2 %all-reduce.41 = (f32[32,32]{0,1:T(8,128)S(1)}, f32[32,32]{0,1:T(8,128)S(1)}, f32[32,32]{1,0:T(8,128)S(1)}) all-reduce(f32[32,32]{0,1:T(8,128)S(1)} %get-tuple-element.189, f32[32,32]{0,1:T(8,128)S(1)} %get-tuple-element.190, f32[32,32]{1,0:T(8,128)S(1)} %get-tuple-element.191), channel_id=1, replica_groups=mesh['gx_0'=4,'gx_1'=4,'gy_0'=4,'gy_1'=2] {'gx_1'}, use_global_device_ids=true, to_apply=%region_14.16 | all-reduce | flops 3072 | bytes 24576 | tf_op jit(solution)/shard_map/psum | solution.py:41
  218.3 11.7 %all-reduce.37 = (f32[32,32]{0,1:T(8,128)S(1)}, f32[32,32]{0,1:T(8,128)S(1)}, f32[32,32]{1,0:T(8,128)S(1)}) all-reduce(f32[32,32]{0,1:T(8,128)S(1)} %get-tuple-element.177, f32[32,32]{0,1:T(8,128)S(1)} %get-tuple-element.178, f32[32,32]{1,0:T(8,128)S(1)} %get-tuple-element.179), channel_id=1, replica_groups=mesh['gx_0'=4,'gx_1'=4,'gy_0'=4,'gy_1'=2] {'gy_0'}, use_global_device_ids=true, to_apply=%region_15.17 | all-reduce | flops 3072 | bytes 24576 | tf_op jit(solution)/shard_map/psum | solution.py:41
  230.0 15.0 %all-reduce.49 = (f32[32,32]{0,1:T(8,128)S(1)}, f32[32,32]{0,1:T(8,128)S(1)}, f32[32,32]{1,0:T(8,128)S(1)}) all-reduce(f32[32,32]{0,1:T(8,128)S(1)} %get-tuple-element.165, f32[32,32]{0,1:T(8,128)S(1)} %get-tuple-element.166, f32[32,32]{1,0:T(8,128)S(1)} %get-tuple-element.167), channel_id=1, replica_groups=mesh['gx_0'=4,'gx_1'=4,'gy_0'=4,'gy_1'=2] {'gy_1'}, use_global_device_ids=true, to_apply=%region_16.18 | all-reduce | flops 3072 | bytes 24576 | tf_op jit(solution)/shard_map/psum | solution.py:41
  288.2 14.5 %all-reduce.44 = (f32[32,32]{0,1:T(8,128)S(1)}, f32[32,32]{1,0:T(8,128)S(1)}, f32[32,32]{1,0:T(8,128)S(1)}) all-reduce(f32[32,32]{0,1:T(8,128)S(1)} %convolution_bitcast_fusion.15, f32[32,32]{1,0:T(8,128)S(1)} %convolution_bitcast_fusion.13, ...), channel_id=1, replica_groups=mesh['gx_0'=4,'gx_1'=4,'gy_0'=4,'gy_1'=2] {'gx_0'}, use_global_device_ids=true, to_apply=%region_21.24 | all-reduce | flops 3072 | bytes 24576 | tf_op jit(solution)/shard_map/psum | solution.py:41
  302.7 11.6 %all-reduce.40 = (f32[32,32]{0,1:T(8,128)S(1)}, f32[32,32]{1,0:T(8,128)S(1)}, f32[32,32]{1,0:T(8,128)S(1)}) all-reduce(f32[32,32]{0,1:T(8,128)S(1)} %get-tuple-element.186, f32[32,32]{1,0:T(8,128)S(1)} %get-tuple-element.187, f32[32,32]{1,0:T(8,128)S(1)} %get-tuple-element.188), channel_id=1, replica_groups=mesh['gx_0'=4,'gx_1'=4,'gy_0'=4,'gy_1'=2] {'gx_1'}, use_global_device_ids=true, to_apply=%region_22.25 | all-reduce | flops 3072 | bytes 24576 | tf_op jit(solution)/shard_map/psum | solution.py:41
  314.4 11.2 %all-reduce.36 = (f32[32,32]{0,1:T(8,128)S(1)}, f32[32,32]{1,0:T(8,128)S(1)}, f32[32,32]{1,0:T(8,128)S(1)}) all-reduce(f32[32,32]{0,1:T(8,128)S(1)} %get-tuple-element.174, f32[32,32]{1,0:T(8,128)S(1)} %get-tuple-element.175, f32[32,32]{1,0:T(8,128)S(1)} %get-tuple-element.176), channel_id=1, replica_groups=mesh['gx_0'=4,'gx_1'=4,'gy_0'=4,'gy_1'=2] {'gy_0'}, use_global_device_ids=true, to_apply=%region_23.26 | all-reduce | flops 3072 | bytes 24576 | tf_op jit(solution)/shard_map/psum | solution.py:41
  325.6 15.0 %all-reduce.48 = (f32[32,32]{0,1:T(8,128)S(1)}, f32[32,32]{1,0:T(8,128)S(1)}, f32[32,32]{1,0:T(8,128)S(1)}) all-reduce(f32[32,32]{0,1:T(8,128)S(1)} %get-tuple-element.162, f32[32,32]{1,0:T(8,128)S(1)} %get-tuple-element.163, f32[32,32]{1,0:T(8,128)S(1)} %get-tuple-element.164), channel_id=1, replica_groups=mesh['gx_0'=4,'gx_1'=4,'gy_0'=4,'gy_1'=2] {'gy_1'}, use_global_device_ids=true, to_apply=%region_24.27 | all-reduce | flops 3072 | bytes 24576 | tf_op jit(solution)/shard_map/psum | solution.py:41
  363.9 16.0 %psum.440 = f32[32,32]{0,1:T(8,128)S(1)} all-reduce(f32[32,32]{0,1:T(8,128)S(1)} %convolution_bitcast_fusion.11), channel_id=1, replica_groups=mesh['gx_0'=4,'gx_1'=4,'gy_0'=4,'gy_1'=2] {'gx_0'}, use_global_device_ids=true, to_apply=%region_33.36 | all-reduce | flops 1024 | bytes 8192 | tf_op jit(solution)/shard_map/psum | solution.py:41
  401.4 15.2 %psum.443 = f32[32,32]{0,1:T(8,128)S(1)} all-reduce(f32[32,32]{0,1:T(8,128)S(1)} %psum.442), channel_id=1, replica_groups=mesh['gx_0'=4,'gx_1'=4,'gy_0'=4,'gy_1'=2] {'gy_1'}, use_global_device_ids=true, to_apply=%region_36.39 | all-reduce | flops 1024 | bytes 8192 | tf_op jit(solution)/shard_map/psum | solution.py:41
  452.9 18.1 %all-reduce.43 = (f32[32,32]{0,1:T(8,128)S(1)}, f32[32,32]{0,1:T(8,128)S(1)}, f32[32,32]{1,0:T(8,128)S(1)}) all-reduce(f32[32,32]{0,1:T(8,128)S(1)} %convolution_bitcast_fusion.8, f32[32,32]{0,1:T(8,128)S(1)} %convolution_bitcast_fusion.9, ...), channel_id=1, replica_groups=mesh['gx_0'=4,'gx_1'=4,'gy_0'=4,'gy_1'=2] {'gx_0'}, use_global_device_ids=true, to_apply=%region_41.44 | all-reduce | flops 3072 | bytes 24576 | tf_op jit(solution)/shard_map/psum | solution.py:41
  471.0 11.2 %all-reduce.39 = (f32[32,32]{0,1:T(8,128)S(1)}, f32[32,32]{0,1:T(8,128)S(1)}, f32[32,32]{1,0:T(8,128)S(1)}) all-reduce(f32[32,32]{0,1:T(8,128)S(1)} %get-tuple-element.183, f32[32,32]{0,1:T(8,128)S(1)} %get-tuple-element.184, f32[32,32]{1,0:T(8,128)S(1)} %get-tuple-element.185), channel_id=1, replica_groups=mesh['gx_0'=4,'gx_1'=4,'gy_0'=4,'gy_1'=2] {'gx_1'}, use_global_device_ids=true, to_apply=%region_42.45 | all-reduce | flops 3072 | bytes 24576 | tf_op jit(solution)/shard_map/psum | solution.py:41
  482.3 11.2 %all-reduce.35 = (f32[32,32]{0,1:T(8,128)S(1)}, f32[32,32]{0,1:T(8,128)S(1)}, f32[32,32]{1,0:T(8,128)S(1)}) all-reduce(f32[32,32]{0,1:T(8,128)S(1)} %get-tuple-element.171, f32[32,32]{0,1:T(8,128)S(1)} %get-tuple-element.172, f32[32,32]{1,0:T(8,128)S(1)} %get-tuple-element.173), channel_id=1, replica_groups=mesh['gx_0'=4,'gx_1'=4,'gy_0'=4,'gy_1'=2] {'gy_0'}, use_global_device_ids=true, to_apply=%region_43.46 | all-reduce | flops 3072 | bytes 24576 | tf_op jit(solution)/shard_map/psum | solution.py:41
  493.5 15.2 %all-reduce.47 = (f32[32,32]{0,1:T(8,128)S(1)}, f32[32,32]{0,1:T(8,128)S(1)}, f32[32,32]{1,0:T(8,128)S(1)}) all-reduce(f32[32,32]{0,1:T(8,128)S(1)} %get-tuple-element.159, f32[32,32]{0,1:T(8,128)S(1)} %get-tuple-element.160, f32[32,32]{1,0:T(8,128)S(1)} %get-tuple-element.161), channel_id=1, replica_groups=mesh['gx_0'=4,'gx_1'=4,'gy_0'=4,'gy_1'=2] {'gy_1'}, use_global_device_ids=true, to_apply=%region_44.47 | all-reduce | flops 3072 | bytes 24576 | tf_op jit(solution)/shard_map/psum | solution.py:41
  552.3 14.3 %all-reduce.42 = (f32[32,32]{0,1:T(8,128)S(1)}, f32[32,32]{1,0:T(8,128)S(1)}, f32[32,32]{1,0:T(8,128)S(1)}) all-reduce(f32[32,32]{0,1:T(8,128)S(1)} %convolution_bitcast_fusion.5, f32[32,32]{1,0:T(8,128)S(1)} %convolution_bitcast_fusion.3, ...), channel_id=1, replica_groups=mesh['gx_0'=4,'gx_1'=4,'gy_0'=4,'gy_1'=2] {'gx_0'}, use_global_device_ids=true, to_apply=%region_49.52 | all-reduce | flops 3072 | bytes 24576 | tf_op jit(solution)/shard_map/psum | solution.py:41
  566.6 12.1 %all-reduce.38 = (f32[32,32]{0,1:T(8,128)S(1)}, f32[32,32]{1,0:T(8,128)S(1)}, f32[32,32]{1,0:T(8,128)S(1)}) all-reduce(f32[32,32]{0,1:T(8,128)S(1)} %get-tuple-element.180, f32[32,32]{1,0:T(8,128)S(1)} %get-tuple-element.181, f32[32,32]{1,0:T(8,128)S(1)} %get-tuple-element.182), channel_id=1, replica_groups=mesh['gx_0'=4,'gx_1'=4,'gy_0'=4,'gy_1'=2] {'gx_1'}, use_global_device_ids=true, to_apply=%region_50.53 | all-reduce | flops 3072 | bytes 24576 | tf_op jit(solution)/shard_map/psum | solution.py:41
  578.7 11.2 %all-reduce.34 = (f32[32,32]{0,1:T(8,128)S(1)}, f32[32,32]{1,0:T(8,128)S(1)}, f32[32,32]{1,0:T(8,128)S(1)}) all-reduce(f32[32,32]{0,1:T(8,128)S(1)} %get-tuple-element.168, f32[32,32]{1,0:T(8,128)S(1)} %get-tuple-element.169, f32[32,32]{1,0:T(8,128)S(1)} %get-tuple-element.170), channel_id=1, replica_groups=mesh['gx_0'=4,'gx_1'=4,'gy_0'=4,'gy_1'=2] {'gy_0'}, use_global_device_ids=true, to_apply=%region_51.54 | all-reduce | flops 3072 | bytes 24576 | tf_op jit(solution)/shard_map/psum | solution.py:41
  590.0 15.0 %all-reduce.46 = (f32[32,32]{0,1:T(8,128)S(1)}, f32[32,32]{1,0:T(8,128)S(1)}, f32[32,32]{1,0:T(8,128)S(1)}) all-reduce(f32[32,32]{0,1:T(8,128)S(1)} %get-tuple-element.156, f32[32,32]{1,0:T(8,128)S(1)} %get-tuple-element.157, f32[32,32]{1,0:T(8,128)S(1)} %get-tuple-element.158), channel_id=1, replica_groups=mesh['gx_0'=4,'gx_1'=4,'gy_0'=4,'gy_1'=2] {'gy_1'}, use_global_device_ids=true, to_apply=%region_52.55 | all-reduce | flops 3072 | bytes 24576 | tf_op jit(solution)/shard_map/psum | solution.py:41
  628.4 15.4 %psum.468 = f32[32,32]{0,1:T(8,128)S(1)} all-reduce(f32[32,32]{0,1:T(8,128)S(1)} %convolution_bitcast_fusion.1), channel_id=1, replica_groups=mesh['gx_0'=4,'gx_1'=4,'gy_0'=4,'gy_1'=2] {'gx_0'}, use_global_device_ids=true, to_apply=%region_61.64 | all-reduce | flops 1024 | bytes 8192 | tf_op jit(solution)/shard_map/psum | solution.py:41
  665.4 15.2 %psum.471 = f32[32,32]{0,1:T(8,128)S(1)} all-reduce(f32[32,32]{0,1:T(8,128)S(1)} %psum.470), channel_id=1, replica_groups=mesh['gx_0'=4,'gx_1'=4,'gy_0'=4,'gy_1'=2] {'gy_1'}, use_global_device_ids=true, to_apply=%region_64.67 | all-reduce | flops 1024 | bytes 8192 | tf_op jit(solution)/shard_map/psum | solution.py:41
  (362 shorter events, 345.2 us)
Async XLA Ops:
  40.8 68.6 %all-to-all-start = ((bf16[64,128,128]{2,0,1:T(8,128)(2,1)}), bf16[64,128,128]{2,0,1:T(8,128)(2,1)S(1)}, u32[]{:S(2)}, u32[]{:S(2)}) async-start(bf16[64,128,128]{2,0,1:T(8,128)(2,1)} %copy.199), calls=%async_computation | async-start | bytes 4194304 | tf_op jit(solution)/shard_map/all_to_all | solution.py:103
  53.3 53.5 %collective-permute-start.2 = (f32[32,4,1,128]{3,0,2,1:T(8,128)}, f32[32,4,1,128]{3,0,2,1:T(8,128)S(1)}, u32[]{:S(2)}, u32[]{:S(2)}) collective-permute-start(f32[32,4,1,128]{3,0,2,1:T(8,128)} %get-tuple-element.251), channel_id=1, source_target_pairs={{0,8},{8,16},{16,24},{24,32},{32,40},{40,48},{48,56},{56,64},{64,7... | collective-permute-start | bytes 196616 | tf_op jit(solution)/shard_map/ppermute | solution.py:22
  56.6 52.2 %collective-permute-start = (f32[32,4,1,128]{3,0,2,1:T(8,128)S(1)}, f32[32,4,1,128]{3,0,2,1:T(8,128)S(1)}, u32[]{:S(2)}, u32[]{:S(2)}) collective-permute-start(f32[32,4,1,128]{3,0,2,1:T(8,128)S(1)} %get-tuple-element.250), channel_id=1, source_target_pairs={{8,0},{16,8},{24,16},{32,24},{40,32},{48,40},{56,48},{64,56},{72,6... | collective-permute-start | bytes 196616 | tf_op jit(solution)/shard_map/ppermute | solution.py:23
  58.6 43.8 %collective-permute-start.4 = (f32[4,8,1]{2,1,0:T(8,128)}, f32[4,8,1]{2,1,0:T(8,128)}, u32[]{:S(2)}, u32[]{:S(2)}) collective-permute-start(f32[4,8,1]{2,1,0:T(8,128)} %slice.379), channel_id=1, source_target_pairs={{0,1},{1,2},{2,3},{3,4},{4,5},{5,6},{6,7},{8,9},{9,10},{10,11},{11... | collective-permute-start | bytes 392 | tf_op jit(solution)/shard_map/ppermute | solution.py:37
  62.4 44.4 %collective-permute-start.1 = (f32[4,1,128]{2,1,0:T(1,128)S(1)}, f32[4,1,128]{2,1,0:T(1,128)S(1)}, u32[]{:S(2)}, u32[]{:S(2)}) collective-permute-start(f32[4,1,128]{2,1,0:T(1,128)S(1)} %slice.373), channel_id=1, source_target_pairs={{0,8},{8,16},{16,24},{24,32},{32,40},{40,48},{48,56},{56,64},{64,7... | collective-permute-start | bytes 6152 | tf_op jit(solution)/shard_map/ppermute | solution.py:37
  67.8 105.9 %collective-permute-start.3 = (f32[32,4,8,1]{3,0,2,1:T(8,128)}, f32[32,4,8,1]{3,0,2,1:T(8,128)}, u32[]{:S(2)}, u32[]{:S(2)}) collective-permute-start(f32[32,4,8,1]{3,0,2,1:T(8,128)} %get-tuple-element.248), channel_id=1, source_target_pairs={{1,0},{2,1},{3,2},{4,3},{5,4},{6,5},{7,6},{9,8},{10,9},{11,10},{12... | collective-permute-start | bytes 12296 | tf_op jit(solution)/shard_map/ppermute | solution.py:23
  102.4 71.4 %collective-permute-start.5 = (f32[32,4,8,1]{3,0,2,1:T(8,128)}, f32[32,4,8,1]{3,0,2,1:T(8,128)}, u32[]{:S(2)}, u32[]{:S(2)}) collective-permute-start(f32[32,4,8,1]{3,0,2,1:T(8,128)} %get-tuple-element.249), channel_id=1, source_target_pairs={{0,1},{1,2},{2,3},{3,4},{4,5},{5,6},{6,7},{8,9},{9,10},{10,11},{11... | collective-permute-start | bytes 12296 | tf_op jit(solution)/shard_map/ppermute | solution.py:22
  109.4 20.2 %all-to-all-start.1 = ((s32[1,128,128]{2,0,1:T(1,128)}), s32[1,128,128]{2,0,1:T(1,128)S(1)}, u32[]{:S(2)}, u32[]{:S(2)}) async-start(s32[1,128,128]{2,0,1:T(1,128)} %bitcast.5), calls=%async_computation.1 | async-start | bytes 131072 | tf_op jit(solution)/shard_map/all_to_all | solution.py:104
  176.3 12.1 %collective-permute-start.8 = (f32[32,4,8,1]{3,0,2,1:T(8,128)S(1)}, f32[32,4,8,1]{3,0,2,1:T(8,128)S(1)}, u32[]{:S(2)}, u32[]{:S(2)}) collective-permute-start(f32[32,4,8,1]{3,0,2,1:T(8,128)S(1)} %get-tuple-element.242), channel_id=1, source_target_pairs={{1,0},{2,1},{3,2},{4,3},{5,4},{6,5},{7,6},{9,8},{10,9},{11,10},{12... | collective-permute-start | bytes 12296 | tf_op jit(solution)/shard_map/ppermute | solution.py:23
  179.4 9.0 %collective-permute-start.9 = (f32[32,4,8,1]{3,0,2,1:T(8,128)S(1)}, f32[32,4,8,1]{3,0,2,1:T(8,128)S(1)}, u32[]{:S(2)}, u32[]{:S(2)}) collective-permute-start(f32[32,4,8,1]{3,0,2,1:T(8,128)S(1)} %get-tuple-element.243), channel_id=1, source_target_pairs={{0,1},{1,2},{2,3},{3,4},{4,5},{5,6},{6,7},{8,9},{9,10},{10,11},{11... | collective-permute-start | bytes 12296 | tf_op jit(solution)/shard_map/ppermute | solution.py:22
  269.8 14.1 %collective-permute-start.12 = (f32[32,4,8,1]{3,0,2,1:T(8,128)}, f32[32,4,8,1]{3,0,2,1:T(8,128)S(1)}, u32[]{:S(2)}, u32[]{:S(2)}) collective-permute-start(f32[32,4,8,1]{3,0,2,1:T(8,128)} %get-tuple-element.236), channel_id=1, source_target_pairs={{1,0},{2,1},{3,2},{4,3},{5,4},{6,5},{7,6},{9,8},{10,9},{11,10},{12... | collective-permute-start | bytes 12296 | tf_op jit(solution)/shard_map/ppermute | solution.py:23
  271.9 12.0 %collective-permute-start.13 = (f32[32,4,8,1]{3,0,2,1:T(8,128)}, f32[32,4,8,1]{3,0,2,1:T(8,128)}, u32[]{:S(2)}, u32[]{:S(2)}) collective-permute-start(f32[32,4,8,1]{3,0,2,1:T(8,128)} %get-tuple-element.237), channel_id=1, source_target_pairs={{0,1},{1,2},{2,3},{3,4},{4,5},{5,6},{6,7},{8,9},{9,10},{10,11},{11... | collective-permute-start | bytes 12296 | tf_op jit(solution)/shard_map/ppermute | solution.py:22
  275.4 8.5 %collective-permute-start.10 = (f32[32,4,1,128]{3,0,2,1:T(8,128)}, f32[32,4,1,128]{3,0,2,1:T(8,128)S(1)}, u32[]{:S(2)}, u32[]{:S(2)}) collective-permute-start(f32[32,4,1,128]{3,0,2,1:T(8,128)} %get-tuple-element.239), channel_id=1, source_target_pairs={{8,0},{16,8},{24,16},{32,24},{40,32},{48,40},{56,48},{64,56},{72,6... | collective-permute-start | bytes 196616 | tf_op jit(solution)/shard_map/ppermute | solution.py:23
  350.4 11.6 %collective-permute-start.16 = (f32[32,4,8,1]{3,0,2,1:T(8,128)S(1)}, f32[32,4,8,1]{3,0,2,1:T(8,128)S(1)}, u32[]{:S(2)}, u32[]{:S(2)}) collective-permute-start(f32[32,4,8,1]{3,0,2,1:T(8,128)S(1)} %get-tuple-element.230), channel_id=1, source_target_pairs={{1,0},{2,1},{3,2},{4,3},{5,4},{6,5},{7,6},{9,8},{10,9},{11,10},{12... | collective-permute-start | bytes 12296 | tf_op jit(solution)/shard_map/ppermute | solution.py:23
  352.4 9.6 %collective-permute-start.17 = (f32[32,4,8,1]{3,0,2,1:T(8,128)S(1)}, f32[32,4,8,1]{3,0,2,1:T(8,128)S(1)}, u32[]{:S(2)}, u32[]{:S(2)}) collective-permute-start(f32[32,4,8,1]{3,0,2,1:T(8,128)S(1)} %get-tuple-element.231), channel_id=1, source_target_pairs={{0,1},{1,2},{2,3},{3,4},{4,5},{5,6},{6,7},{8,9},{9,10},{10,11},{11... | collective-permute-start | bytes 12296 | tf_op jit(solution)/shard_map/ppermute | solution.py:22
  424.8 11.3 %collective-permute-start.20 = (f32[32,4,8,1]{3,0,2,1:T(8,128)S(1)}, f32[32,4,8,1]{3,0,2,1:T(8,128)S(1)}, u32[]{:S(2)}, u32[]{:S(2)}) collective-permute-start(f32[32,4,8,1]{3,0,2,1:T(8,128)S(1)} %get-tuple-element.224), channel_id=1, source_target_pairs={{1,0},{2,1},{3,2},{4,3},{5,4},{6,5},{7,6},{9,8},{10,9},{11,10},{12... | collective-permute-start | bytes 12296 | tf_op jit(solution)/shard_map/ppermute | solution.py:23
  426.9 9.6 %collective-permute-start.21 = (f32[32,4,8,1]{3,0,2,1:T(8,128)S(1)}, f32[32,4,8,1]{3,0,2,1:T(8,128)S(1)}, u32[]{:S(2)}, u32[]{:S(2)}) collective-permute-start(f32[32,4,8,1]{3,0,2,1:T(8,128)S(1)} %get-tuple-element.225), channel_id=1, source_target_pairs={{0,1},{1,2},{2,3},{3,4},{4,5},{5,6},{6,7},{8,9},{9,10},{10,11},{11... | collective-permute-start | bytes 12296 | tf_op jit(solution)/shard_map/ppermute | solution.py:22
  438.3 11.9 %collective-permute-start.24 = (f32[32,4,8,1]{3,0,2,1:T(8,128)S(1)}, f32[32,4,8,1]{3,0,2,1:T(8,128)S(1)}, u32[]{:S(2)}, u32[]{:S(2)}) collective-permute-start(f32[32,4,8,1]{3,0,2,1:T(8,128)S(1)} %get-tuple-element.218), channel_id=1, source_target_pairs={{1,0},{2,1},{3,2},{4,3},{5,4},{6,5},{7,6},{9,8},{10,9},{11,10},{12... | collective-permute-start | bytes 12296 | tf_op jit(solution)/shard_map/ppermute | solution.py:23
  440.3 9.9 %collective-permute-start.25 = (f32[32,4,8,1]{3,0,2,1:T(8,128)S(1)}, f32[32,4,8,1]{3,0,2,1:T(8,128)S(1)}, u32[]{:S(2)}, u32[]{:S(2)}) collective-permute-start(f32[32,4,8,1]{3,0,2,1:T(8,128)S(1)} %get-tuple-element.219), channel_id=1, source_target_pairs={{0,1},{1,2},{2,3},{3,4},{4,5},{5,6},{6,7},{8,9},{9,10},{10,11},{11... | collective-permute-start | bytes 12296 | tf_op jit(solution)/shard_map/ppermute | solution.py:22
  533.4 14.6 %collective-permute-start.28 = (f32[32,4,8,1]{3,0,2,1:T(8,128)}, f32[32,4,8,1]{3,0,2,1:T(8,128)S(1)}, u32[]{:S(2)}, u32[]{:S(2)}) collective-permute-start(f32[32,4,8,1]{3,0,2,1:T(8,128)} %get-tuple-element.212), channel_id=1, source_target_pairs={{1,0},{2,1},{3,2},{4,3},{5,4},{6,5},{7,6},{9,8},{10,9},{11,10},{12... | collective-permute-start | bytes 12296 | tf_op jit(solution)/shard_map/ppermute | solution.py:23
  535.5 12.5 %collective-permute-start.29 = (f32[32,4,8,1]{3,0,2,1:T(8,128)}, f32[32,4,8,1]{3,0,2,1:T(8,128)}, u32[]{:S(2)}, u32[]{:S(2)}) collective-permute-start(f32[32,4,8,1]{3,0,2,1:T(8,128)} %get-tuple-element.213), channel_id=1, source_target_pairs={{0,1},{1,2},{2,3},{3,4},{4,5},{5,6},{6,7},{8,9},{9,10},{10,11},{11... | collective-permute-start | bytes 12296 | tf_op jit(solution)/shard_map/ppermute | solution.py:22
  539.0 9.0 %collective-permute-start.26 = (f32[32,4,1,128]{3,0,2,1:T(8,128)}, f32[32,4,1,128]{3,0,2,1:T(8,128)S(1)}, u32[]{:S(2)}, u32[]{:S(2)}) collective-permute-start(f32[32,4,1,128]{3,0,2,1:T(8,128)} %get-tuple-element.215), channel_id=1, source_target_pairs={{8,0},{16,8},{24,16},{32,24},{40,32},{48,40},{56,48},{64,56},{72,6... | collective-permute-start | bytes 196616 | tf_op jit(solution)/shard_map/ppermute | solution.py:23
  614.6 11.6 %collective-permute-start.32 = (f32[32,4,8,1]{3,0,2,1:T(8,128)S(1)}, f32[32,4,8,1]{3,0,2,1:T(8,128)S(1)}, u32[]{:S(2)}, u32[]{:S(2)}) collective-permute-start(f32[32,4,8,1]{3,0,2,1:T(8,128)S(1)} %get-tuple-element.206), channel_id=1, source_target_pairs={{1,0},{2,1},{3,2},{4,3},{5,4},{6,5},{7,6},{9,8},{10,9},{11,10},{12... | collective-permute-start | bytes 12296 | tf_op jit(solution)/shard_map/ppermute | solution.py:23
  616.7 9.6 %collective-permute-start.33 = (f32[32,4,8,1]{3,0,2,1:T(8,128)S(1)}, f32[32,4,8,1]{3,0,2,1:T(8,128)S(1)}, u32[]{:S(2)}, u32[]{:S(2)}) collective-permute-start(f32[32,4,8,1]{3,0,2,1:T(8,128)S(1)} %get-tuple-element.207), channel_id=1, source_target_pairs={{0,1},{1,2},{2,3},{3,4},{4,5},{5,6},{6,7},{8,9},{9,10},{10,11},{11... | collective-permute-start | bytes 12296 | tf_op jit(solution)/shard_map/ppermute | solution.py:22
  (41 other events, 943.5 us)
where the time goes:
time: 702 us; the launch traced here: 691 us
  blocking collectives  321 us (46%)
  starting transfers between devices  117 us (17%)
  other arithmetic  87.7 us (12%)
  local copies, waits for them, and re-layouts  82.2 us (12%)
  matrix products  69.4 us (10%)
  waiting for transfers between devices  11.7 us (2%)
    psum x24, blocking collectives, by_axis(): return functools.reduce(lax.psum, axes, x)  321 us
    ppermute x16, starting transfers between devices, with_halo(): lax.ppermute(last, axis, up)  59.3 us
    dot_general x16, matrix products, add_block(): jnp.dot(piece_values, one_hot, preferred_element_type=jnp.float32)  43 us
    unnamed x63, local copies, waits for them, and re-layouts  38.7 us
    another operation x30, other arithmetic, spd_solve(): factor = jnp.linalg.cholesky(matrix)  35.9 us
    another operation x20, other arithmetic, spd_solve(): return jax.scipy.linalg.cho_solve((factor, True), right)  31.4 us
    ppermute x16, starting transfers between devices, with_halo(): lax.ppermute(initial, axis, [(b, a) for a, b in up])  27.8 us
    scatter x1, local copies, waits for them, and re-layouts, body(): jnp.zeros((currents.shape[0], slots_all), jnp.bfloat16).at[:, slot_index]  23.6 us
  transfers between devices with their start and end apart: 36, of which 9 were waited for; matrix products, arithmetic and copies ran while one was open for 14% of the time, Pallas kernels for 0%

commit v1 on v0

--- a/solution.py
+++ b/solution.py
@@ -101,7 +101,12 @@
     cell_slots = jnp.zeros((1, slots_all), jnp.int32).at[0, slot_index].set(cells)
     arrived, cell_slots = (
         lax.all_to_all(packed, GX_GY, split_axis=1, concat_axis=1, tiled=True),
-        lax.all_to_all(cell_slots, GX_GY, split_axis=1, concat_axis=1, tiled=True),
+        jnp.concatenate(
+            lax.all_to_all(
+                jnp.stack(jnp.split(cell_slots, lax.axis_size(GX_GY), axis=1)), GX_GY, 0, 0
+            ),
+            axis=1,
+        ),
     )
     block_rows = min(1024, slots_all)
     block_count = slots_all // block_rows

time: 702 us -> 771 us (1.098)
  local copies, waits for them, and re-layouts: 82.2 us -> 151 us
    unnamed x63 -> x190, local copies, waits for them, and re-layouts: 38.7 us -> 107 us
  transfers between devices with their start and end apart: 36 -> 36, of which waited for: 9 -> 9; matrix products, arithmetic and copies ran while one was open for 14% -> 21% of each run, Pallas kernels for 0% -> 0%
where the time goes in v1:
time: 771 us; the launch traced here: 761 us
  blocking collectives  321 us (42%)
  local copies, waits for them, and re-layouts  151 us (20%)
  starting transfers between devices  117 us (15%)
  other arithmetic  87.7 us (11%)
  matrix products  69.4 us (9%)
  waiting for transfers between devices  11.7 us (2%)
    psum x24, blocking collectives, by_axis(): return functools.reduce(lax.psum, axes, x)  321 us
    unnamed x190, local copies, waits for them, and re-layouts  107 us
    ppermute x16, starting transfers between devices, with_halo(): lax.ppermute(last, axis, up)  59.2 us
    dot_general x16, matrix products, add_block(): jnp.dot(piece_values, one_hot, preferred_element_type=jnp.float32)  43 us
    another operation x30, other arithmetic, spd_solve(): factor = jnp.linalg.cholesky(matrix)  35.9 us
    another operation x20, other arithmetic, spd_solve(): return jax.scipy.linalg.cho_solve((factor, True), right)  31.4 us
    ppermute x16, starting transfers between devices, with_halo(): lax.ppermute(initial, axis, [(b, a) for a, b in up])  28 us
    scatter x1, local copies, waits for them, and re-layouts, body(): jnp.zeros((currents.shape[0], slots_all), jnp.bfloat16).at[:, slot_index]  23.6 us
  transfers between devices with their start and end apart: 36, of which 9 were waited for; matrix products, arithmetic and copies ran while one was open for 21% of the time, Pallas kernels for 0%

profile of v1, /device:TPU:1, one launch (start us, length us, event | category | flops | bytes accessed | tf_op | source)
XLA Modules:
  0.0 760.7 jit_solution(7004924391856724217)
XLA Ops:
  12.3 23.6 %scatter_custom_fusion = bf16[64,16384]{0,1:T(8,128)(2,1)} fusion(s32[8192]{0:T(1024)S(1)} %bitcast.854, bf16[8192,64]{1,0:T(8,128)(2,1)S(1)} %copy.198, bf16[]{:T(256)} %constant.128.clone.1), kind=kCustom, calls=%fused_computation.18 | custom fusion | bytes 2097154 | tf_op jit(solution)/shard_map/scatter | solution.py:100
  40.8 11.5 %all-to-all-start = ((bf16[64,128,128]{2,0,1:T(8,128)(2,1)}), bf16[64,128,128]{2,0,1:T(8,128)(2,1)S(1)}, u32[]{:S(2)}, u32[]{:S(2)}) async-start(bf16[64,128,128]{2,0,1:T(8,128)(2,1)} %copy.199), calls=%async_computation | async-start | bytes 4194304 | tf_op jit(solution)/shard_map/all_to_all | solution.py:103
  70.1 30.7 %scatter_custom_fusion.1 = s32[16384]{0:T(1024)S(1)} fusion(s32[8192]{0:T(1024)S(1)} %broadcast_select_fusion, s32[8192]{0:T(1024)} %param.26, s32[]{:T(128)} %constant.126.clone.1), kind=kCustom, calls=%fused_computation.418 | custom fusion | bytes 66048
  198.6 43.1 %while.16 = (s32[]{:T(128)}, f32[64,1024]{1,0:T(8,128)}, bf16[64,16384]{1,0:T(8,128)(2,1)}, s32[128,1,128]{2,1,0:T(1,128)S(1)}, s32[]{:T(128)}, /*index=5*/s32[]{:T(128)}, s32[]{:T(128)}, s32[]{:T(128)}) while((s32[]{:T(128)}, f32[64,1024]{1,0:T(8,128)}, bf16[64,16384]{1,0:T(8,128)(2,1)}, s32[128,1,128]{2,1,0:T(1,128)S(1)}, ...), condition=%wide.region_6.7_spmd.clone, body=%wide.region_5.6_spmd.clone.sunk | while | flops 135397376 | bytes 667797 | solution.py:121
  259.3 16.8 %all-reduce.45 = (f32[32,32]{0,1:T(8,128)S(1)}, f32[32,32]{0,1:T(8,128)S(1)}, f32[32,32]{1,0:T(8,128)S(1)}) all-reduce(f32[32,32]{0,1:T(8,128)S(1)} %convolution_bitcast_fusion.18, f32[32,32]{0,1:T(8,128)S(1)} %convolution_bitcast_fusion.19, ...), channel_id=1, replica_groups=mesh['gx_0'=4,'gx_1'=4,'gy_0'=4,'gy_1'=2] {'gx_0'}, use_global_device_ids=true, to_apply=%region_13.15 | all-reduce | flops 3072 | bytes 24576 | tf_op jit(solution)/shard_map/psum | solution.py:41
  276.1 11.2 %all-reduce.41 = (f32[32,32]{0,1:T(8,128)S(1)}, f32[32,32]{0,1:T(8,128)S(1)}, f32[32,32]{1,0:T(8,128)S(1)}) all-reduce(f32[32,32]{0,1:T(8,128)S(1)} %get-tuple-element.189, f32[32,32]{0,1:T(8,128)S(1)} %get-tuple-element.190, f32[32,32]{1,0:T(8,128)S(1)} %get-tuple-element.191), channel_id=1, replica_groups=mesh['gx_0'=4,'gx_1'=4,'gy_0'=4,'gy_1'=2] {'gx_1'}, use_global_device_ids=true, to_apply=%region_14.16 | all-reduce | flops 3072 | bytes 24576 | tf_op jit(solution)/shard_map/psum | solution.py:41
  287.3 11.7 %all-reduce.37 = (f32[32,32]{0,1:T(8,128)S(1)}, f32[32,32]{0,1:T(8,128)S(1)}, f32[32,32]{1,0:T(8,128)S(1)}) all-reduce(f32[32,32]{0,1:T(8,128)S(1)} %get-tuple-element.177, f32[32,32]{0,1:T(8,128)S(1)} %get-tuple-element.178, f32[32,32]{1,0:T(8,128)S(1)} %get-tuple-element.179), channel_id=1, replica_groups=mesh['gx_0'=4,'gx_1'=4,'gy_0'=4,'gy_1'=2] {'gy_0'}, use_global_device_ids=true, to_apply=%region_15.17 | all-reduce | flops 3072 | bytes 24576 | tf_op jit(solution)/shard_map/psum | solution.py:41
  299.0 15.0 %all-reduce.49 = (f32[32,32]{0,1:T(8,128)S(1)}, f32[32,32]{0,1:T(8,128)S(1)}, f32[32,32]{1,0:T(8,128)S(1)}) all-reduce(f32[32,32]{0,1:T(8,128)S(1)} %get-tuple-element.165, f32[32,32]{0,1:T(8,128)S(1)} %get-tuple-element.166, f32[32,32]{1,0:T(8,128)S(1)} %get-tuple-element.167), channel_id=1, replica_groups=mesh['gx_0'=4,'gx_1'=4,'gy_0'=4,'gy_1'=2] {'gy_1'}, use_global_device_ids=true, to_apply=%region_16.18 | all-reduce | flops 3072 | bytes 24576 | tf_op jit(solution)/shard_map/psum | solution.py:41
  357.2 14.7 %all-reduce.44 = (f32[32,32]{0,1:T(8,128)S(1)}, f32[32,32]{1,0:T(8,128)S(1)}, f32[32,32]{1,0:T(8,128)S(1)}) all-reduce(f32[32,32]{0,1:T(8,128)S(1)} %convolution_bitcast_fusion.15, f32[32,32]{1,0:T(8,128)S(1)} %convolution_bitcast_fusion.13, ...), channel_id=1, replica_groups=mesh['gx_0'=4,'gx_1'=4,'gy_0'=4,'gy_1'=2] {'gx_0'}, use_global_device_ids=true, to_apply=%region_21.24 | all-reduce | flops 3072 | bytes 24576 | tf_op jit(solution)/shard_map/psum | solution.py:41
  372.0 11.4 %all-reduce.40 = (f32[32,32]{0,1:T(8,128)S(1)}, f32[32,32]{1,0:T(8,128)S(1)}, f32[32,32]{1,0:T(8,128)S(1)}) all-reduce(f32[32,32]{0,1:T(8,128)S(1)} %get-tuple-element.186, f32[32,32]{1,0:T(8,128)S(1)} %get-tuple-element.187, f32[32,32]{1,0:T(8,128)S(1)} %get-tuple-element.188), channel_id=1, replica_groups=mesh['gx_0'=4,'gx_1'=4,'gy_0'=4,'gy_1'=2] {'gx_1'}, use_global_device_ids=true, to_apply=%region_22.25 | all-reduce | flops 3072 | bytes 24576 | tf_op jit(solution)/shard_map/psum | solution.py:41
  383.4 11.2 %all-reduce.36 = (f32[32,32]{0,1:T(8,128)S(1)}, f32[32,32]{1,0:T(8,128)S(1)}, f32[32,32]{1,0:T(8,128)S(1)}) all-reduce(f32[32,32]{0,1:T(8,128)S(1)} %get-tuple-element.174, f32[32,32]{1,0:T(8,128)S(1)} %get-tuple-element.175, f32[32,32]{1,0:T(8,128)S(1)} %get-tuple-element.176), channel_id=1, replica_groups=mesh['gx_0'=4,'gx_1'=4,'gy_0'=4,'gy_1'=2] {'gy_0'}, use_global_device_ids=true, to_apply=%region_23.26 | all-reduce | flops 3072 | bytes 24576 | tf_op jit(solution)/shard_map/psum | solution.py:41
  394.6 15.1 %all-reduce.48 = (f32[32,32]{0,1:T(8,128)S(1)}, f32[32,32]{1,0:T(8,128)S(1)}, f32[32,32]{1,0:T(8,128)S(1)}) all-reduce(f32[32,32]{0,1:T(8,128)S(1)} %get-tuple-element.162, f32[32,32]{1,0:T(8,128)S(1)} %get-tuple-element.163, f32[32,32]{1,0:T(8,128)S(1)} %get-tuple-element.164), channel_id=1, replica_groups=mesh['gx_0'=4,'gx_1'=4,'gy_0'=4,'gy_1'=2] {'gy_1'}, use_global_device_ids=true, to_apply=%region_24.27 | all-reduce | flops 3072 | bytes 24576 | tf_op jit(solution)/shard_map/psum | solution.py:41
  432.9 16.2 %psum.440 = f32[32,32]{0,1:T(8,128)S(1)} all-reduce(f32[32,32]{0,1:T(8,128)S(1)} %convolution_bitcast_fusion.11), channel_id=1, replica_groups=mesh['gx_0'=4,'gx_1'=4,'gy_0'=4,'gy_1'=2] {'gx_0'}, use_global_device_ids=true, to_apply=%region_33.36 | all-reduce | flops 1024 | bytes 8192 | tf_op jit(solution)/shard_map/psum | solution.py:41
  470.7 15.2 %psum.443 = f32[32,32]{0,1:T(8,128)S(1)} all-reduce(f32[32,32]{0,1:T(8,128)S(1)} %psum.442), channel_id=1, replica_groups=mesh['gx_0'=4,'gx_1'=4,'gy_0'=4,'gy_1'=2] {'gy_1'}, use_global_device_ids=true, to_apply=%region_36.39 | all-reduce | flops 1024 | bytes 8192 | tf_op jit(solution)/shard_map/psum | solution.py:41
  522.2 18.0 %all-reduce.43 = (f32[32,32]{0,1:T(8,128)S(1)}, f32[32,32]{0,1:T(8,128)S(1)}, f32[32,32]{1,0:T(8,128)S(1)}) all-reduce(f32[32,32]{0,1:T(8,128)S(1)} %convolution_bitcast_fusion.8, f32[32,32]{0,1:T(8,128)S(1)} %convolution_bitcast_fusion.9, ...), channel_id=1, replica_groups=mesh['gx_0'=4,'gx_1'=4,'gy_0'=4,'gy_1'=2] {'gx_0'}, use_global_device_ids=true, to_apply=%region_41.44 | all-reduce | flops 3072 | bytes 24576 | tf_op jit(solution)/shard_map/psum | solution.py:41
  540.2 11.2 %all-reduce.39 = (f32[32,32]{0,1:T(8,128)S(1)}, f32[32,32]{0,1:T(8,128)S(1)}, f32[32,32]{1,0:T(8,128)S(1)}) all-reduce(f32[32,32]{0,1:T(8,128)S(1)} %get-tuple-element.183, f32[32,32]{0,1:T(8,128)S(1)} %get-tuple-element.184, f32[32,32]{1,0:T(8,128)S(1)} %get-tuple-element.185), channel_id=1, replica_groups=mesh['gx_0'=4,'gx_1'=4,'gy_0'=4,'gy_1'=2] {'gx_1'}, use_global_device_ids=true, to_apply=%region_42.45 | all-reduce | flops 3072 | bytes 24576 | tf_op jit(solution)/shard_map/psum | solution.py:41
  551.5 11.2 %all-reduce.35 = (f32[32,32]{0,1:T(8,128)S(1)}, f32[32,32]{0,1:T(8,128)S(1)}, f32[32,32]{1,0:T(8,128)S(1)}) all-reduce(f32[32,32]{0,1:T(8,128)S(1)} %get-tuple-element.171, f32[32,32]{0,1:T(8,128)S(1)} %get-tuple-element.172, f32[32,32]{1,0:T(8,128)S(1)} %get-tuple-element.173), channel_id=1, replica_groups=mesh['gx_0'=4,'gx_1'=4,'gy_0'=4,'gy_1'=2] {'gy_0'}, use_global_device_ids=true, to_apply=%region_43.46 | all-reduce | flops 3072 | bytes 24576 | tf_op jit(solution)/shard_map/psum | solution.py:41
  562.7 15.2 %all-reduce.47 = (f32[32,32]{0,1:T(8,128)S(1)}, f32[32,32]{0,1:T(8,128)S(1)}, f32[32,32]{1,0:T(8,128)S(1)}) all-reduce(f32[32,32]{0,1:T(8,128)S(1)} %get-tuple-element.159, f32[32,32]{0,1:T(8,128)S(1)} %get-tuple-element.160, f32[32,32]{1,0:T(8,128)S(1)} %get-tuple-element.161), channel_id=1, replica_groups=mesh['gx_0'=4,'gx_1'=4,'gy_0'=4,'gy_1'=2] {'gy_1'}, use_global_device_ids=true, to_apply=%region_44.47 | all-reduce | flops 3072 | bytes 24576 | tf_op jit(solution)/shard_map/psum | solution.py:41
  621.5 14.3 %all-reduce.42 = (f32[32,32]{0,1:T(8,128)S(1)}, f32[32,32]{1,0:T(8,128)S(1)}, f32[32,32]{1,0:T(8,128)S(1)}) all-reduce(f32[32,32]{0,1:T(8,128)S(1)} %convolution_bitcast_fusion.5, f32[32,32]{1,0:T(8,128)S(1)} %convolution_bitcast_fusion.3, ...), channel_id=1, replica_groups=mesh['gx_0'=4,'gx_1'=4,'gy_0'=4,'gy_1'=2] {'gx_0'}, use_global_device_ids=true, to_apply=%region_49.52 | all-reduce | flops 3072 | bytes 24576 | tf_op jit(solution)/shard_map/psum | solution.py:41
  635.8 12.1 %all-reduce.38 = (f32[32,32]{0,1:T(8,128)S(1)}, f32[32,32]{1,0:T(8,128)S(1)}, f32[32,32]{1,0:T(8,128)S(1)}) all-reduce(f32[32,32]{0,1:T(8,128)S(1)} %get-tuple-element.180, f32[32,32]{1,0:T(8,128)S(1)} %get-tuple-element.181, f32[32,32]{1,0:T(8,128)S(1)} %get-tuple-element.182), channel_id=1, replica_groups=mesh['gx_0'=4,'gx_1'=4,'gy_0'=4,'gy_1'=2] {'gx_1'}, use_global_device_ids=true, to_apply=%region_50.53 | all-reduce | flops 3072 | bytes 24576 | tf_op jit(solution)/shard_map/psum | solution.py:41
  647.9 11.2 %all-reduce.34 = (f32[32,32]{0,1:T(8,128)S(1)}, f32[32,32]{1,0:T(8,128)S(1)}, f32[32,32]{1,0:T(8,128)S(1)}) all-reduce(f32[32,32]{0,1:T(8,128)S(1)} %get-tuple-element.168, f32[32,32]{1,0:T(8,128)S(1)} %get-tuple-element.169, f32[32,32]{1,0:T(8,128)S(1)} %get-tuple-element.170), channel_id=1, replica_groups=mesh['gx_0'=4,'gx_1'=4,'gy_0'=4,'gy_1'=2] {'gy_0'}, use_global_device_ids=true, to_apply=%region_51.54 | all-reduce | flops 3072 | bytes 24576 | tf_op jit(solution)/shard_map/psum | solution.py:41
  659.2 15.0 %all-reduce.46 = (f32[32,32]{0,1:T(8,128)S(1)}, f32[32,32]{1,0:T(8,128)S(1)}, f32[32,32]{1,0:T(8,128)S(1)}) all-reduce(f32[32,32]{0,1:T(8,128)S(1)} %get-tuple-element.156, f32[32,32]{1,0:T(8,128)S(1)} %get-tuple-element.157, f32[32,32]{1,0:T(8,128)S(1)} %get-tuple-element.158), channel_id=1, replica_groups=mesh['gx_0'=4,'gx_1'=4,'gy_0'=4,'gy_1'=2] {'gy_1'}, use_global_device_ids=true, to_apply=%region_52.55 | all-reduce | flops 3072 | bytes 24576 | tf_op jit(solution)/shard_map/psum | solution.py:41
  697.6 15.4 %psum.468 = f32[32,32]{0,1:T(8,128)S(1)} all-reduce(f32[32,32]{0,1:T(8,128)S(1)} %convolution_bitcast_fusion.1), channel_id=1, replica_groups=mesh['gx_0'=4,'gx_1'=4,'gy_0'=4,'gy_1'=2] {'gx_0'}, use_global_device_ids=true, to_apply=%region_61.64 | all-reduce | flops 1024 | bytes 8192 | tf_op jit(solution)/shard_map/psum | solution.py:41
  734.6 15.2 %psum.471 = f32[32,32]{0,1:T(8,128)S(1)} all-reduce(f32[32,32]{0,1:T(8,128)S(1)} %psum.470), channel_id=1, replica_groups=mesh['gx_0'=4,'gx_1'=4,'gy_0'=4,'gy_1'=2] {'gy_1'}, use_global_device_ids=true, to_apply=%region_64.67 | all-reduce | flops 1024 | bytes 8192 | tf_op jit(solution)/shard_map/psum | solution.py:41
  (490 shorter events, 414.7 us)
Async XLA Ops:
  40.8 137.9 %all-to-all-start = ((bf16[64,128,128]{2,0,1:T(8,128)(2,1)}), bf16[64,128,128]{2,0,1:T(8,128)(2,1)S(1)}, u32[]{:S(2)}, u32[]{:S(2)}) async-start(bf16[64,128,128]{2,0,1:T(8,128)(2,1)} %copy.199), calls=%async_computation | async-start | bytes 4194304 | tf_op jit(solution)/shard_map/all_to_all | solution.py:103
  53.3 122.8 %collective-permute-start.2 = (f32[32,4,1,128]{3,0,2,1:T(8,128)}, f32[32,4,1,128]{3,0,2,1:T(8,128)S(1)}, u32[]{:S(2)}, u32[]{:S(2)}) collective-permute-start(f32[32,4,1,128]{3,0,2,1:T(8,128)} %get-tuple-element.251), channel_id=1, source_target_pairs={{0,8},{8,16},{16,24},{24,32},{32,40},{40,48},{48,56},{56,64},{64,7... | collective-permute-start | bytes 196616 | tf_op jit(solution)/shard_map/ppermute | solution.py:22
  56.6 121.4 %collective-permute-start = (f32[32,4,1,128]{3,0,2,1:T(8,128)S(1)}, f32[32,4,1,128]{3,0,2,1:T(8,128)S(1)}, u32[]{:S(2)}, u32[]{:S(2)}) collective-permute-start(f32[32,4,1,128]{3,0,2,1:T(8,128)S(1)} %get-tuple-element.250), channel_id=1, source_target_pairs={{8,0},{16,8},{24,16},{32,24},{40,32},{48,40},{56,48},{64,56},{72,6... | collective-permute-start | bytes 196616 | tf_op jit(solution)/shard_map/ppermute | solution.py:23
  58.6 112.9 %collective-permute-start.4 = (f32[4,8,1]{2,1,0:T(8,128)}, f32[4,8,1]{2,1,0:T(8,128)}, u32[]{:S(2)}, u32[]{:S(2)}) collective-permute-start(f32[4,8,1]{2,1,0:T(8,128)} %slice.379), channel_id=1, source_target_pairs={{0,1},{1,2},{2,3},{3,4},{4,5},{5,6},{6,7},{8,9},{9,10},{10,11},{11... | collective-permute-start | bytes 392 | tf_op jit(solution)/shard_map/ppermute | solution.py:37
  62.4 113.7 %collective-permute-start.1 = (f32[4,1,128]{2,1,0:T(1,128)S(1)}, f32[4,1,128]{2,1,0:T(1,128)S(1)}, u32[]{:S(2)}, u32[]{:S(2)}) collective-permute-start(f32[4,1,128]{2,1,0:T(1,128)S(1)} %slice.373), channel_id=1, source_target_pairs={{0,8},{8,16},{16,24},{24,32},{32,40},{40,48},{48,56},{56,64},{64,7... | collective-permute-start | bytes 6152 | tf_op jit(solution)/shard_map/ppermute | solution.py:37
  67.8 174.9 %collective-permute-start.3 = (f32[32,4,8,1]{3,0,2,1:T(8,128)}, f32[32,4,8,1]{3,0,2,1:T(8,128)}, u32[]{:S(2)}, u32[]{:S(2)}) collective-permute-start(f32[32,4,8,1]{3,0,2,1:T(8,128)} %get-tuple-element.248), channel_id=1, source_target_pairs={{1,0},{2,1},{3,2},{4,3},{5,4},{6,5},{7,6},{9,8},{10,9},{11,10},{12... | collective-permute-start | bytes 12296 | tf_op jit(solution)/shard_map/ppermute | solution.py:23
  171.5 71.3 %collective-permute-start.5 = (f32[32,4,8,1]{3,0,2,1:T(8,128)}, f32[32,4,8,1]{3,0,2,1:T(8,128)}, u32[]{:S(2)}, u32[]{:S(2)}) collective-permute-start(f32[32,4,8,1]{3,0,2,1:T(8,128)} %get-tuple-element.249), channel_id=1, source_target_pairs={{0,1},{1,2},{2,3},{3,4},{4,5},{5,6},{6,7},{8,9},{9,10},{10,11},{11... | collective-permute-start | bytes 12296 | tf_op jit(solution)/shard_map/ppermute | solution.py:22
  178.7 19.9 %all-to-all-start.1 = ((s32[128,1,128]{2,1,0:T(1,128)}), s32[128,1,128]{2,1,0:T(1,128)S(1)}, u32[]{:S(2)}, u32[]{:S(2)}) async-start(s32[128,1,128]{2,1,0:T(1,128)} %constant_dynamic-update-slice_fusion), calls=%async_computation.1 | async-start | bytes 131072 | tf_op jit(solution)/shard_map/all_to_all | solution.py:105
  245.3 12.1 %collective-permute-start.8 = (f32[32,4,8,1]{3,0,2,1:T(8,128)S(1)}, f32[32,4,8,1]{3,0,2,1:T(8,128)S(1)}, u32[]{:S(2)}, u32[]{:S(2)}) collective-permute-start(f32[32,4,8,1]{3,0,2,1:T(8,128)S(1)} %get-tuple-element.242), channel_id=1, source_target_pairs={{1,0},{2,1},{3,2},{4,3},{5,4},{6,5},{7,6},{9,8},{10,9},{11,10},{12... | collective-permute-start | bytes 12296 | tf_op jit(solution)/shard_map/ppermute | solution.py:23
  248.4 9.0 %collective-permute-start.9 = (f32[32,4,8,1]{3,0,2,1:T(8,128)S(1)}, f32[32,4,8,1]{3,0,2,1:T(8,128)S(1)}, u32[]{:S(2)}, u32[]{:S(2)}) collective-permute-start(f32[32,4,8,1]{3,0,2,1:T(8,128)S(1)} %get-tuple-element.243), channel_id=1, source_target_pairs={{0,1},{1,2},{2,3},{3,4},{4,5},{5,6},{6,7},{8,9},{9,10},{10,11},{11... | collective-permute-start | bytes 12296 | tf_op jit(solution)/shard_map/ppermute | solution.py:22
  338.8 14.1 %collective-permute-start.12 = (f32[32,4,8,1]{3,0,2,1:T(8,128)}, f32[32,4,8,1]{3,0,2,1:T(8,128)S(1)}, u32[]{:S(2)}, u32[]{:S(2)}) collective-permute-start(f32[32,4,8,1]{3,0,2,1:T(8,128)} %get-tuple-element.236), channel_id=1, source_target_pairs={{1,0},{2,1},{3,2},{4,3},{5,4},{6,5},{7,6},{9,8},{10,9},{11,10},{12... | collective-permute-start | bytes 12296 | tf_op jit(solution)/shard_map/ppermute | solution.py:23
  340.9 12.0 %collective-permute-start.13 = (f32[32,4,8,1]{3,0,2,1:T(8,128)}, f32[32,4,8,1]{3,0,2,1:T(8,128)}, u32[]{:S(2)}, u32[]{:S(2)}) collective-permute-start(f32[32,4,8,1]{3,0,2,1:T(8,128)} %get-tuple-element.237), channel_id=1, source_target_pairs={{0,1},{1,2},{2,3},{3,4},{4,5},{5,6},{6,7},{8,9},{9,10},{10,11},{11... | collective-permute-start | bytes 12296 | tf_op jit(solution)/shard_map/ppermute | solution.py:22
  344.4 8.5 %collective-permute-start.10 = (f32[32,4,1,128]{3,0,2,1:T(8,128)}, f32[32,4,1,128]{3,0,2,1:T(8,128)S(1)}, u32[]{:S(2)}, u32[]{:S(2)}) collective-permute-start(f32[32,4,1,128]{3,0,2,1:T(8,128)} %get-tuple-element.239), channel_id=1, source_target_pairs={{8,0},{16,8},{24,16},{32,24},{40,32},{48,40},{56,48},{64,56},{72,6... | collective-permute-start | bytes 196616 | tf_op jit(solution)/shard_map/ppermute | solution.py:23
  419.4 11.6 %collective-permute-start.16 = (f32[32,4,8,1]{3,0,2,1:T(8,128)S(1)}, f32[32,4,8,1]{3,0,2,1:T(8,128)S(1)}, u32[]{:S(2)}, u32[]{:S(2)}) collective-permute-start(f32[32,4,8,1]{3,0,2,1:T(8,128)S(1)} %get-tuple-element.230), channel_id=1, source_target_pairs={{1,0},{2,1},{3,2},{4,3},{5,4},{6,5},{7,6},{9,8},{10,9},{11,10},{12... | collective-permute-start | bytes 12296 | tf_op jit(solution)/shard_map/ppermute | solution.py:23
  421.5 9.6 %collective-permute-start.17 = (f32[32,4,8,1]{3,0,2,1:T(8,128)S(1)}, f32[32,4,8,1]{3,0,2,1:T(8,128)S(1)}, u32[]{:S(2)}, u32[]{:S(2)}) collective-permute-start(f32[32,4,8,1]{3,0,2,1:T(8,128)S(1)} %get-tuple-element.231), channel_id=1, source_target_pairs={{0,1},{1,2},{2,3},{3,4},{4,5},{5,6},{6,7},{8,9},{9,10},{10,11},{11... | collective-permute-start | bytes 12296 | tf_op jit(solution)/shard_map/ppermute | solution.py:22
  494.0 11.3 %collective-permute-start.20 = (f32[32,4,8,1]{3,0,2,1:T(8,128)S(1)}, f32[32,4,8,1]{3,0,2,1:T(8,128)S(1)}, u32[]{:S(2)}, u32[]{:S(2)}) collective-permute-start(f32[32,4,8,1]{3,0,2,1:T(8,128)S(1)} %get-tuple-element.224), channel_id=1, source_target_pairs={{1,0},{2,1},{3,2},{4,3},{5,4},{6,5},{7,6},{9,8},{10,9},{11,10},{12... | collective-permute-start | bytes 12296 | tf_op jit(solution)/shard_map/ppermute | solution.py:23
  496.1 9.6 %collective-permute-start.21 = (f32[32,4,8,1]{3,0,2,1:T(8,128)S(1)}, f32[32,4,8,1]{3,0,2,1:T(8,128)S(1)}, u32[]{:S(2)}, u32[]{:S(2)}) collective-permute-start(f32[32,4,8,1]{3,0,2,1:T(8,128)S(1)} %get-tuple-element.225), channel_id=1, source_target_pairs={{0,1},{1,2},{2,3},{3,4},{4,5},{5,6},{6,7},{8,9},{9,10},{10,11},{11... | collective-permute-start | bytes 12296 | tf_op jit(solution)/shard_map/ppermute | solution.py:22
  507.5 11.9 %collective-permute-start.24 = (f32[32,4,8,1]{3,0,2,1:T(8,128)S(1)}, f32[32,4,8,1]{3,0,2,1:T(8,128)S(1)}, u32[]{:S(2)}, u32[]{:S(2)}) collective-permute-start(f32[32,4,8,1]{3,0,2,1:T(8,128)S(1)} %get-tuple-element.218), channel_id=1, source_target_pairs={{1,0},{2,1},{3,2},{4,3},{5,4},{6,5},{7,6},{9,8},{10,9},{11,10},{12... | collective-permute-start | bytes 12296 | tf_op jit(solution)/shard_map/ppermute | solution.py:23
  509.5 9.9 %collective-permute-start.25 = (f32[32,4,8,1]{3,0,2,1:T(8,128)S(1)}, f32[32,4,8,1]{3,0,2,1:T(8,128)S(1)}, u32[]{:S(2)}, u32[]{:S(2)}) collective-permute-start(f32[32,4,8,1]{3,0,2,1:T(8,128)S(1)} %get-tuple-element.219), channel_id=1, source_target_pairs={{0,1},{1,2},{2,3},{3,4},{4,5},{5,6},{6,7},{8,9},{9,10},{10,11},{11... | collective-permute-start | bytes 12296 | tf_op jit(solution)/shard_map/ppermute | solution.py:22
  602.6 14.6 %collective-permute-start.28 = (f32[32,4,8,1]{3,0,2,1:T(8,128)}, f32[32,4,8,1]{3,0,2,1:T(8,128)S(1)}, u32[]{:S(2)}, u32[]{:S(2)}) collective-permute-start(f32[32,4,8,1]{3,0,2,1:T(8,128)} %get-tuple-element.212), channel_id=1, source_target_pairs={{1,0},{2,1},{3,2},{4,3},{5,4},{6,5},{7,6},{9,8},{10,9},{11,10},{12... | collective-permute-start | bytes 12296 | tf_op jit(solution)/shard_map/ppermute | solution.py:23
  604.7 12.5 %collective-permute-start.29 = (f32[32,4,8,1]{3,0,2,1:T(8,128)}, f32[32,4,8,1]{3,0,2,1:T(8,128)}, u32[]{:S(2)}, u32[]{:S(2)}) collective-permute-start(f32[32,4,8,1]{3,0,2,1:T(8,128)} %get-tuple-element.213), channel_id=1, source_target_pairs={{0,1},{1,2},{2,3},{3,4},{4,5},{5,6},{6,7},{8,9},{9,10},{10,11},{11... | collective-permute-start | bytes 12296 | tf_op jit(solution)/shard_map/ppermute | solution.py:22
  608.2 9.0 %collective-permute-start.26 = (f32[32,4,1,128]{3,0,2,1:T(8,128)}, f32[32,4,1,128]{3,0,2,1:T(8,128)S(1)}, u32[]{:S(2)}, u32[]{:S(2)}) collective-permute-start(f32[32,4,1,128]{3,0,2,1:T(8,128)} %get-tuple-element.215), channel_id=1, source_target_pairs={{8,0},{16,8},{24,16},{32,24},{40,32},{48,40},{56,48},{64,56},{72,6... | collective-permute-start | bytes 196616 | tf_op jit(solution)/shard_map/ppermute | solution.py:23
  683.8 11.6 %collective-permute-start.32 = (f32[32,4,8,1]{3,0,2,1:T(8,128)S(1)}, f32[32,4,8,1]{3,0,2,1:T(8,128)S(1)}, u32[]{:S(2)}, u32[]{:S(2)}) collective-permute-start(f32[32,4,8,1]{3,0,2,1:T(8,128)S(1)} %get-tuple-element.206), channel_id=1, source_target_pairs={{1,0},{2,1},{3,2},{4,3},{5,4},{6,5},{7,6},{9,8},{10,9},{11,10},{12... | collective-permute-start | bytes 12296 | tf_op jit(solution)/shard_map/ppermute | solution.py:23
  686.0 9.6 %collective-permute-start.33 = (f32[32,4,8,1]{3,0,2,1:T(8,128)S(1)}, f32[32,4,8,1]{3,0,2,1:T(8,128)S(1)}, u32[]{:S(2)}, u32[]{:S(2)}) collective-permute-start(f32[32,4,8,1]{3,0,2,1:T(8,128)S(1)} %get-tuple-element.207), channel_id=1, source_target_pairs={{0,1},{1,2},{2,3},{3,4},{4,5},{5,6},{6,7},{8,9},{9,10},{10,11},{11... | collective-permute-start | bytes 12296 | tf_op jit(solution)/shard_map/ppermute | solution.py:22
  (41 other events, 1081.9 us)
